TPU v7x, 128 devices: a whole 4x4x4 slice. The times are simulated.
128 devices in a mesh: ctx: 8 (over x_hi, y), tile: 16 (over z, x_lo, core).
Axes of the slice: x: 4 (x_hi: 2, x_lo: 2; x = x_hi * 2 + x_lo), y: 4, z: 4, core: 2. Of those that a mesh axis runs over, the one named last changes fastest.
Arguments:
- syndrome_bits: int32 [8, 2, 64, 512], P(None, None, 'ctx', 'tile'), may hold values from 0 to 1
- region_assign: int32 [32, 256], P('ctx', 'tile'), may hold values from 0 to 127
- state_in: bfloat16 [64, 512, 512], P('ctx', 'tile'), may hold values from -3 to 3
- bit_to_candidate: float32 [2, 512], replicated, may hold values from -5 to 5
- bit_to_gate: float32 [2, 512], replicated, may hold values from -5 to 5
- conv_weight: bfloat16 [9, 512, 512], replicated, may hold values from -0.09375 to 0.09375
- gate_weight: bfloat16 [512, 512], replicated, may hold values from -0.25 to 0.25
- gate_bias: float32 [512], replicated, may hold values from -4 to 1
- pool_weight: bfloat16 [512, 1024], replicated, may hold values from -0.25 to 0.25
- region_embed: bfloat16 [1024, 1024], P('ctx'), may hold values from -6 to 6
- attn_norm_gain: float32 [1024], replicated, may hold values from 0.1 to 1.9
- query_weight: bfloat16 [1024, 1024], replicated
- key_weight: bfloat16 [1024, 1024], replicated
- value_weight: bfloat16 [1024, 1024], replicated, may hold values from -0.1875 to 0.1875
- out_weight: bfloat16 [1024, 1024], replicated, may hold values from -0.1875 to 0.1875
- mlp_norm_gain: float32 [1024], replicated, may hold values from 0.1 to 1.9
- mlp_up: bfloat16 [1024, 2048], replicated, may hold values from -0.1875 to 0.1875
- mlp_down: bfloat16 [2048, 1024], replicated, may hold values from -0.125 to 0.125
- return_weight: bfloat16 [1024, 512], replicated, may hold values from -0.1875 to 0.1875
Outputs:
- state_out: bfloat16 [64, 512, 512], P('ctx', 'tile')
- context_out: bfloat16 [1024, 1024], P('ctx')
All inputs are finite; a program needn't handle non-finite values.
Results may differ from a plain program's by a relative error of at most 0.02.
Values may be sent and summed in bfloat16 or wider, within the bound.
A program may use at most 128 MiB of HBM per device.

v0:
```python
import math
import jax
import jax.numpy as jnp
from jax import lax
from jax.sharding import PartitionSpec as P

HEADS = 8
HDIM = 128
ROUNDS = 8


def extended(value, sides, width):
    for axis, dim in sides:
        size, length = (lax.axis_size(axis), value.shape[dim])
        up = [(i, (i + 1) % size) for i in range(size - 1)]
        down = [(j, i) for i, j in up]
        last = lax.slice_in_dim(value, length - width, length, axis=dim)
        first = lax.slice_in_dim(value, 0, width, axis=dim)
        before = lax.ppermute(last, axis, up)
        after = lax.ppermute(first, axis, down)
        value = jnp.concatenate([before, value, after], axis=dim)
    return value


def rms_norm(values, gain):
    return values * lax.rsqrt(jnp.mean(values * values, axis=-1, keepdims=True) + 1e-05) * gain


def advance(
    state, padded, syndrome_now, conv_flat, gate_weight, gate_bias, bit_to_candidate, bit_to_gate
):
    patch_rows, patch_cols, channels = state.shape
    rounded = padded[1 : patch_rows + 1, 1 : patch_cols + 1]
    columns = jnp.concatenate(
        [
            padded[offset_row : offset_row + patch_rows, offset_col : offset_col + patch_cols]
            for offset_row in range(3)
            for offset_col in range(3)
        ],
        axis=-1,
    )
    syndrome_flags = syndrome_now.astype(jnp.float32)
    drive_cand = (
        syndrome_flags[0][..., None] * bit_to_candidate[0]
        + syndrome_flags[1][..., None] * bit_to_candidate[1]
    )
    drive_gate = (
        syndrome_flags[0][..., None] * bit_to_gate[0]
        + syndrome_flags[1][..., None] * bit_to_gate[1]
    )
    candidate = (
        jnp.dot(
            columns.reshape(patch_rows * patch_cols, 9 * channels),
            conv_flat,
            preferred_element_type=jnp.float32,
        ).reshape(patch_rows, patch_cols, channels)
        + drive_cand
    )
    update_gate = jax.nn.sigmoid(
        jnp.dot(
            rounded.reshape(patch_rows * patch_cols, channels),
            gate_weight,
            preferred_element_type=jnp.float32,
        ).reshape(patch_rows, patch_cols, channels)
        + drive_gate
        + gate_bias
    )
    return state + update_gate * (jnp.tanh(candidate) - state)


def region_layer(
    tokens,
    attn_norm_gain,
    query_weight,
    key_weight,
    value_weight,
    out_weight,
    mlp_norm_gain,
    mlp_up,
    mlp_down,
    gather_keys,
):
    token_count = tokens.shape[0]
    normed = rms_norm(tokens, attn_norm_gain).astype(jnp.bfloat16)
    queries = jnp.dot(normed, query_weight, preferred_element_type=jnp.float32).astype(jnp.bfloat16)
    query_heads = queries.reshape(token_count, HEADS, HDIM).transpose(1, 0, 2)
    key_rows = jnp.dot(normed, key_weight, preferred_element_type=jnp.float32).astype(jnp.bfloat16)
    value_rows = jnp.dot(normed, value_weight, preferred_element_type=jnp.float32).astype(
        jnp.bfloat16
    )
    scale = 1.0 / math.sqrt(HDIM)

    def absorb(running, gathered, first_row):
        running_max, denominator, weighted = running
        key_part, value_part = gathered
        part_rows = key_part.shape[0]
        scores = (
            jnp.einsum(
                "hqd,khd->hqk",
                query_heads,
                key_part.reshape(part_rows, HEADS, HDIM),
                preferred_element_type=jnp.float32,
            )
            * scale
        )
        new_max = jnp.maximum(running_max, jnp.max(scores, axis=-1))
        weights = jnp.exp(scores - new_max[..., None])
        denominator = jnp.sum(weights, axis=-1)
        weighted = jnp.einsum(
            "hqk,khd->hqd",
            weights.astype(jnp.bfloat16),
            value_part.reshape(part_rows, HEADS, HDIM),
            preferred_element_type=jnp.float32,
        )
        return (new_max, denominator, weighted)

    start_state = (
        jnp.full((HEADS, token_count), -1e30, jnp.float32),
        jnp.zeros((HEADS, token_count), jnp.float32),
        jnp.zeros((HEADS, token_count, HDIM), jnp.float32),
    )
    running_max, denominator, weighted = gather_keys(key_rows, value_rows, absorb, start_state)
    attention = (
        (weighted / denominator[..., None])
        .transpose(1, 0, 2)
        .reshape(token_count, HEADS * HDIM)
        .astype(jnp.bfloat16)
    )
    attended = tokens + jnp.dot(attention, out_weight, preferred_element_type=jnp.float32)
    hidden = jax.nn.gelu(
        jnp.dot(
            rms_norm(attended, mlp_norm_gain).astype(jnp.bfloat16),
            mlp_up,
            preferred_element_type=jnp.float32,
        )
    ).astype(jnp.bfloat16)
    return (attended + jnp.dot(hidden, mlp_down, preferred_element_type=jnp.float32)).astype(
        jnp.bfloat16
    )


def local(
    syndrome_bits,
    region_assign,
    state_in,
    bit_to_candidate,
    bit_to_gate,
    conv_weight,
    gate_weight,
    gate_bias,
    pool_weight,
    region_embed,
    attn_norm_gain,
    query_weight,
    key_weight,
    value_weight,
    out_weight,
    mlp_norm_gain,
    mlp_up,
    mlp_down,
    return_weight,
):
    state = state_in.astype(jnp.float32)
    patch_rows, patch_cols, channels = state.shape
    conv_flat = conv_weight.reshape(9 * channels, channels)
    layer_weights = (
        attn_norm_gain,
        query_weight,
        key_weight,
        value_weight,
        out_weight,
        mlp_norm_gain,
        mlp_up,
        mlp_down,
    )
    context_out = None
    for round_index in range(ROUNDS):
        if round_index == ROUNDS // 2:
            pooled = (
                state.reshape(patch_rows // 2, 2, patch_cols // 2, 2, channels)
                .mean(axis=(1, 3))
                .astype(jnp.bfloat16)
            )
            band_tokens = region_embed.shape[0]
            member = (
                region_assign.reshape(1, -1) == jnp.arange(band_tokens, dtype=jnp.int32)[:, None]
            ).astype(jnp.float32)
            projected = jnp.dot(
                pooled.reshape(-1, channels), pool_weight, preferred_element_type=jnp.float32
            )
            partial_value = jnp.dot(member, projected, precision=lax.Precision.HIGHEST)
            share_rows = band_tokens // lax.axis_size("tile")
            first_row = lax.axis_index("tile") * share_rows
            summed = lax.psum_scatter(
                partial_value.astype(jnp.bfloat16), "tile", scatter_dimension=0, tiled=True
            ).astype(jnp.float32)
            embed_rows = lax.dynamic_slice_in_dim(region_embed, first_row, share_rows, 0).astype(
                jnp.float32
            )
            tokens = summed + embed_rows

            def gather_split(key_rows, value_rows, absorb, start_state):
                return absorb(
                    start_state,
                    (
                        lax.all_gather(key_rows, ("ctx", "tile"), axis=0, tiled=True),
                        lax.all_gather(value_rows, ("ctx", "tile"), axis=0, tiled=True),
                    ),
                    jnp.int32(0),
                )

            local_context = region_layer(tokens, *layer_weights, gather_split)
            context_out = lax.all_gather(local_context, "tile", axis=0, tiled=True)
            returned = jnp.dot(context_out, return_weight, preferred_element_type=jnp.float32)
            share_back = jnp.dot(member.T, returned, precision=lax.Precision.HIGHEST).reshape(
                patch_rows // 2, patch_cols // 2, channels
            )
            state = (
                state.reshape(patch_rows // 2, 2, patch_cols // 2, 2, channels)
                + share_back[:, None, :, None, :]
            ).reshape(patch_rows, patch_cols, channels)
        rounded = state.astype(jnp.bfloat16)
        padded = extended(rounded, (("ctx", 0), ("tile", 1)), 1)
        state = advance(
            state,
            padded,
            syndrome_bits[round_index],
            conv_flat,
            gate_weight,
            gate_bias,
            bit_to_candidate,
            bit_to_gate,
        )
    return (state.astype(jnp.bfloat16), context_out)


def solution(mesh):
    return jax.shard_map(
        local,
        mesh=mesh,
        in_specs=(
            P(None, None, "ctx", "tile"),
            P("ctx", "tile"),
            P("ctx", "tile", None),
            P(),
            P(),
            P(),
            P(),
            P(),
            P(),
            P("ctx", None),
            P(),
            P(),
            P(),
            P(),
            P(),
            P(),
            P(),
            P(),
            P(),
        ),
        out_specs=(P("ctx", "tile", None), P("ctx", None)),
        check_vma=False,
    )
```

profile of v0, /device:TPU:56, one launch (start us, length us, event | category | flops | bytes accessed | tf_op | source)
XLA Modules:
  0.0 692.4 jit_solution(17125236643354716497)
XLA Ops:
  8.2 2.6 collective-permute-start.1
  10.8 6.8 collective-permute-start
  23.0 4.5 collective-permute-start.3
  31.9 7.8 %collective-permute-start.4 = (bf16[1,32,512]{2,1,0:T(8,128)(2,1)S(1)}, bf16[1,32,512]{2,1,0:T(8,128)(2,1)S(1)}, u32[]{:S(2)}, u32[]{:S(2)}) collective-permute-start(bf16[1,32,512]{2,1,0:T(8,128)(2,1)S(1)} %get-tuple-element.46), channel_id=1, source_target_pairs={{0,16},{16,32},{32,48},{48,64},{64,80},{80,96},{96,112},{1,17},{17... | collective-permute-start | bytes 98312 | tf_op jit(solution)/shard_map/ppermute | solution.py:19
  41.6 7.5 %collective-permute-done.5 = bf16[1,32,512]{2,1,0:T(8,128)(2,1)S(1)} collective-permute-done((bf16[1,32,512]{2,1,0:T(8,128)(2,1)S(1)}, bf16[1,32,512]{2,1,0:T(8,128)(2,1)S(1)}, u32[]{:S(2)}, u32[]{:S(2)}) %collective-permute-start.5) | collective-permute-done | bytes 32800 | tf_op jit(solution)/shard_map/ppermute | solution.py:20
  53.5 3.7 collective-permute-done.6
  62.2 3.3 collective-permute-start.9
  65.5 6.1 collective-permute-done.9
  76.0 3.6 collective-permute-done.10
  84.7 3.9 collective-permute-start.13
  88.7 5.5 collective-permute-done.13
  98.6 3.5 collective-permute-done.14
  103.3 3.8 fusion.71
  111.0 53.7 %reduce-scatter.2.cloned.1.call-done = bf16[8,1024]{1,0:T(8,128)(2,1)} async-done(((bf16[128,1024]{1,0:T(8,128)(2,1)}), bf16[8,1024]{1,0:T(8,128)(2,1)}) %reduce-scatter.2.cloned.1.call-update) | async-done | bytes 16400 | tf_op jit(solution)/shard_map/reduce_scatter | solution.py:194
  171.8 196.5 %all-gather.3.cloned.1.call-done = bf16[1024,1024]{1,0:T(8,128)(2,1)} async-done(((bf16[8,1024]{1,0:T(8,128)(2,1)}), bf16[1024,1024]{1,0:T(8,128)(2,1)}) %all-gather.3.cloned.1.call-update) | async-done | bytes 2097168 | tf_op jit(solution)/shard_map/all_gather | solution.py:206
  371.2 193.8 %all-gather.5.cloned.1.call-done = bf16[1024,1024]{1,0:T(8,128)(2,1)} async-done(((bf16[8,1024]{1,0:T(8,128)(2,1)}), bf16[1024,1024]{1,0:T(8,128)(2,1)}) %all-gather.5.cloned.1.call-update) | async-done | bytes 2097168 | tf_op jit(solution)/shard_map/all_gather | solution.py:207
  565.0 3.2 multiply_reduce_fusion
  568.2 4.8 fusion.88
  572.9 17.0 %all_gather.11 = bf16[128,1024]{1,0:T(8,128)(2,1)S(1)} all-gather(bf16[8,1024]{1,0:T(8,128)(2,1)S(1)} %fusion.88), channel_id=1, replica_groups=mesh['ctx'=8,'tile'=16] {'tile'}, dimensions={0}, use_global_device_ids=true | all-gather | bytes 278528 | tf_op jit(solution)/shard_map/all_gather | solution.py:213
  591.2 5.2 collective-permute-start.16
  598.3 7.5 %collective-permute-done.17 = bf16[1,32,512]{2,1,0:T(8,128)(2,1)S(1)} collective-permute-done((bf16[1,32,512]{2,1,0:T(8,128)(2,1)S(1)}, bf16[1,32,512]{2,1,0:T(8,128)(2,1)S(1)}, u32[]{:S(2)}, u32[]{:S(2)}) %collective-permute-start.17) | collective-permute-done | bytes 32800 | tf_op jit(solution)/shard_map/ppermute | solution.py:20
  610.2 3.6 collective-permute-done.18
  614.4 3.9 fusion.69
  621.2 3.4 collective-permute-start.21
  624.6 6.1 collective-permute-done.21
  635.0 3.6 collective-permute-done.22
  643.0 3.9 collective-permute-start.25
  646.9 5.5 collective-permute-done.25
  656.8 3.6 collective-permute-done.26
  664.7 3.9 collective-permute-start.29
  668.6 5.5 collective-permute-done.29
  678.5 3.6 collective-permute-done.30
  (223 shorter events, 86.6 us)
Async XLA Ops:
  7.2 157.5 %reduce-scatter.2.cloned.1.call-start = ((), (), s32[]{:S(2)}) async-start(), calls=%async_computation.1 | async-start | bytes 278528 | tf_op jit(solution)/shard_map/reduce_scatter | solution.py:194
  8.2 12.0 %collective-permute-start.1 = (bf16[1,32,512]{2,1,0:T(8,128)(2,1)S(1)}, bf16[1,32,512]{2,1,0:T(8,128)(2,1)S(1)}, u32[]{:S(2)}, u32[]{:S(2)}) collective-permute-start(bf16[1,32,512]{2,1,0:T(8,128)(2,1)S(1)} %get-tuple-element.48), channel_id=1, source_target_pairs={{16,0},{32,16},{48,32},{64,48},{80,64},{96,80},{112,96},{17,1},{33... | collective-permute-start | bytes 98312 | tf_op jit(solution)/shard_map/ppermute | solution.py:20
  10.8 8.4 %collective-permute-start = (bf16[1,32,512]{2,1,0:T(8,128)(2,1)S(1)}, bf16[1,32,512]{2,1,0:T(8,128)(2,1)S(1)}, u32[]{:S(2)}, u32[]{:S(2)}) collective-permute-start(bf16[1,32,512]{2,1,0:T(8,128)(2,1)S(1)} %get-tuple-element.49), channel_id=1, source_target_pairs={{0,16},{16,32},{32,48},{48,64},{64,80},{80,96},{96,112},{1,17},{17... | collective-permute-start | bytes 98312 | tf_op jit(solution)/shard_map/ppermute | solution.py:19
  20.3 7.2 %collective-permute-start.2 = (bf16[10,1,512]{2,1,0:T(2,128)(2,1)S(1)}, bf16[10,1,512]{2,1,0:T(2,128)(2,1)S(1)}, u32[]{:S(2)}, u32[]{:S(2)}) collective-permute-start(bf16[10,1,512]{2,1,0:T(2,128)(2,1)S(1)} %get-tuple-element.33), channel_id=1, source_target_pairs={{0,1},{1,2},{2,3},{3,4},{4,5},{5,6},{6,7},{7,8},{8,9},{9,10},{10,1... | collective-permute-start | bytes 30728 | tf_op jit(solution)/shard_map/ppermute | solution.py:19
  23.0 6.0 collective-permute-start.3
  31.9 9.7 %collective-permute-start.4 = (bf16[1,32,512]{2,1,0:T(8,128)(2,1)S(1)}, bf16[1,32,512]{2,1,0:T(8,128)(2,1)S(1)}, u32[]{:S(2)}, u32[]{:S(2)}) collective-permute-start(bf16[1,32,512]{2,1,0:T(8,128)(2,1)S(1)} %get-tuple-element.46), channel_id=1, source_target_pairs={{0,16},{16,32},{32,48},{48,64},{64,80},{80,96},{96,112},{1,17},{17... | collective-permute-start | bytes 98312 | tf_op jit(solution)/shard_map/ppermute | solution.py:19
  39.7 9.4 %collective-permute-start.5 = (bf16[1,32,512]{2,1,0:T(8,128)(2,1)S(1)}, bf16[1,32,512]{2,1,0:T(8,128)(2,1)S(1)}, u32[]{:S(2)}, u32[]{:S(2)}) collective-permute-start(bf16[1,32,512]{2,1,0:T(8,128)(2,1)S(1)} %get-tuple-element.47), channel_id=1, source_target_pairs={{16,0},{32,16},{48,32},{64,48},{80,64},{96,80},{112,96},{17,1},{33... | collective-permute-start | bytes 98312 | tf_op jit(solution)/shard_map/ppermute | solution.py:20
  49.2 4.4 collective-permute-start.7
  51.2 6.0 collective-permute-start.6
  59.6 5.9 collective-permute-start.8
  62.2 9.4 %collective-permute-start.9 = (bf16[1,32,512]{2,1,0:T(8,128)(2,1)S(1)}, bf16[1,32,512]{2,1,0:T(8,128)(2,1)S(1)}, u32[]{:S(2)}, u32[]{:S(2)}) collective-permute-start(bf16[1,32,512]{2,1,0:T(8,128)(2,1)S(1)} %get-tuple-element.45), channel_id=1, source_target_pairs={{16,0},{32,16},{48,32},{64,48},{80,64},{96,80},{112,96},{17,1},{33... | collective-permute-start | bytes 98312 | tf_op jit(solution)/shard_map/ppermute | solution.py:20
  71.6 4.4 collective-permute-start.11
  73.6 6.0 collective-permute-start.10
  82.8 5.8 collective-permute-start.12
  84.7 9.4 %collective-permute-start.13 = (bf16[1,32,512]{2,1,0:T(8,128)(2,1)S(1)}, bf16[1,32,512]{2,1,0:T(8,128)(2,1)S(1)}, u32[]{:S(2)}, u32[]{:S(2)}) collective-permute-start(bf16[1,32,512]{2,1,0:T(8,128)(2,1)S(1)} %get-tuple-element.43), channel_id=1, source_target_pairs={{16,0},{32,16},{48,32},{64,48},{80,64},{96,80},{112,96},{17,1},{33... | collective-permute-start | bytes 98312 | tf_op jit(solution)/shard_map/ppermute | solution.py:20
  94.2 4.4 collective-permute-start.15
  96.1 6.0 collective-permute-start.14
  110.9 257.5 %all-gather.3.cloned.1.call-start = ((), (), s32[]{:S(2)}) async-start(), calls=%async_computation.2 | async-start | bytes 2113536 | tf_op jit(solution)/shard_map/all_gather | solution.py:206
  169.0 396.0 %all-gather.5.cloned.1.call-start = ((), (), s32[]{:S(2)}) async-start(), calls=%async_computation.3 | async-start | bytes 2113536 | tf_op jit(solution)/shard_map/all_gather | solution.py:207
  591.2 7.1 %collective-permute-start.16 = (bf16[1,32,512]{2,1,0:T(8,128)(2,1)S(1)}, bf16[1,32,512]{2,1,0:T(8,128)(2,1)S(1)}, u32[]{:S(2)}, u32[]{:S(2)}) collective-permute-start(bf16[1,32,512]{2,1,0:T(8,128)(2,1)S(1)} %get-tuple-element.40), channel_id=1, source_target_pairs={{0,16},{16,32},{32,48},{48,64},{64,80},{80,96},{96,112},{1,17},{17... | collective-permute-start | bytes 98312 | tf_op jit(solution)/shard_map/ppermute | solution.py:19
  596.4 9.4 %collective-permute-start.17 = (bf16[1,32,512]{2,1,0:T(8,128)(2,1)S(1)}, bf16[1,32,512]{2,1,0:T(8,128)(2,1)S(1)}, u32[]{:S(2)}, u32[]{:S(2)}) collective-permute-start(bf16[1,32,512]{2,1,0:T(8,128)(2,1)S(1)} %get-tuple-element.41), channel_id=1, source_target_pairs={{16,0},{32,16},{48,32},{64,48},{80,64},{96,80},{112,96},{17,1},{33... | collective-permute-start | bytes 98312 | tf_op jit(solution)/shard_map/ppermute | solution.py:20
  607.8 6.0 collective-permute-start.18
  618.7 5.9 collective-permute-start.20
  621.2 9.4 %collective-permute-start.21 = (bf16[1,32,512]{2,1,0:T(8,128)(2,1)S(1)}, bf16[1,32,512]{2,1,0:T(8,128)(2,1)S(1)}, u32[]{:S(2)}, u32[]{:S(2)}) collective-permute-start(bf16[1,32,512]{2,1,0:T(8,128)(2,1)S(1)} %get-tuple-element.39), channel_id=1, source_target_pairs={{16,0},{32,16},{48,32},{64,48},{80,64},{96,80},{112,96},{17,1},{33... | collective-permute-start | bytes 98312 | tf_op jit(solution)/shard_map/ppermute | solution.py:20
  630.7 4.4 collective-permute-start.23
  632.6 6.0 collective-permute-start.22
  641.0 5.9 collective-permute-start.24
  643.0 9.4 %collective-permute-start.25 = (bf16[1,32,512]{2,1,0:T(8,128)(2,1)S(1)}, bf16[1,32,512]{2,1,0:T(8,128)(2,1)S(1)}, u32[]{:S(2)}, u32[]{:S(2)}) collective-permute-start(bf16[1,32,512]{2,1,0:T(8,128)(2,1)S(1)} %get-tuple-element.37), channel_id=1, source_target_pairs={{16,0},{32,16},{48,32},{64,48},{80,64},{96,80},{112,96},{17,1},{33... | collective-permute-start | bytes 98312 | tf_op jit(solution)/shard_map/ppermute | solution.py:20
  654.4 6.0 collective-permute-start.26
  662.8 5.9 collective-permute-start.28
  664.7 9.4 %collective-permute-start.29 = (bf16[1,32,512]{2,1,0:T(8,128)(2,1)S(1)}, bf16[1,32,512]{2,1,0:T(8,128)(2,1)S(1)}, u32[]{:S(2)}, u32[]{:S(2)}) collective-permute-start(bf16[1,32,512]{2,1,0:T(8,128)(2,1)S(1)} %get-tuple-element.35), channel_id=1, source_target_pairs={{16,0},{32,16},{48,32},{64,48},{80,64},{96,80},{112,96},{17,1},{33... | collective-permute-start | bytes 98312 | tf_op jit(solution)/shard_map/ppermute | solution.py:20
  676.1 6.0 collective-permute-start.30
  (19 other events, 1146.5 us)
Sparse Core Ops, SparseCore 0:
  111.0 53.6 reduce-scatter.1
  169.1 199.2 all-gather.2
  370.7 194.2 all-gather.4
where the time goes:
time: 694 us; the launch traced here: 692 us
  waiting for transfers between devices  513 us (74%)
  starting transfers between devices  92.5 us (13%)
  matrix products  39.9 us (6%)
  blocking collectives  17 us (2%)
  between operations  15.2 us (2%)
  local copies, waits for them, and re-layouts  8.39 us (1%)
    all_gather x1, waiting for transfers between devices, gather_split(): lax.all_gather(key_rows, ('ctx', 'tile'), axis=0, tiled=True)  197 us
    all_gather x1, waiting for transfers between devices, gather_split(): lax.all_gather(value_rows, ('ctx', 'tile'), axis=0, tiled=True)  194 us
    reduce_scatter x1, waiting for transfers between devices, local(): lax.psum_scatter(partial_value.astype(jnp.bfloat16), 'tile', scatter_dime...  53.7 us
    ppermute x16, starting transfers between devices, extended(): before = lax.ppermute(last, axis, up)  49.2 us
    ppermute x16, waiting for transfers between devices, extended(): after = lax.ppermute(first, axis, down)  43.8 us
    ppermute x16, starting transfers between devices, extended(): after = lax.ppermute(first, axis, down)  43 us
    ppermute x16, waiting for transfers between devices, extended(): before = lax.ppermute(last, axis, up)  25 us
    all_gather x1, blocking collectives, local(): context_out = lax.all_gather(local_context, 'tile', axis=0, tiled=True)  17 us
  transfers between devices with their start and end apart: 35, of which 18 were waited for; matrix products, arithmetic and copies ran while one was open for 1% of the time, Pallas kernels for 0%

commit v1 on v0

--- a/solution.py
+++ b/solution.py
@@ -203,7 +203,15 @@
                 return absorb(
                     start_state,
                     (
-                        lax.all_gather(key_rows, ("ctx", "tile"), axis=0, tiled=True),
+                        jnp.concatenate(
+                            lax.all_to_all(
+                                jnp.stack([key_rows] * lax.axis_size(("ctx", "tile"))),
+                                ("ctx", "tile"),
+                                0,
+                                0,
+                            ),
+                            axis=0,
+                        ),
                         lax.all_gather(value_rows, ("ctx", "tile"), axis=0, tiled=True),
                     ),
                     jnp.int32(0),

time: 694 us -> 512 us (0.74)
  waiting for transfers between devices: 513 us -> 262 us
  blocking collectives: 17 us -> 61.4 us
  starting transfers between devices: 92.5 us -> 113 us
    all_gather x1 -> x0, waiting for transfers between devices: 197 us -> none  [gather_split(): lax.all_gather(key_rows, ('ctx', 'tile'), axis=0, tiled=True)]
    all_to_all x0 -> x1, blocking collectives: none -> 41.8 us  [gather_split(): lax.all_to_all(jnp.stack([key_rows] * lax.axis_size(('ctx', 'tile'))), ('...]
    ppermute x16, waiting for transfers between devices: 43.8 us -> 5.19 us  [extended(): after = lax.ppermute(first, axis, down)]
    all_gather x1, waiting for transfers between devices: 194 us -> 163 us  [gather_split(): lax.all_gather(value_rows, ('ctx', 'tile'), axis=0, tiled=True)]
    ppermute x16, starting transfers between devices: 49.2 us -> 77.3 us  [extended(): before = lax.ppermute(last, axis, up)]
    ppermute x16, waiting for transfers between devices: 25 us -> 36.8 us  [extended(): before = lax.ppermute(last, axis, up)]
    ppermute x16, starting transfers between devices: 43 us -> 35.2 us  [extended(): after = lax.ppermute(first, axis, down)]
  transfers between devices with their start and end apart: 35 -> 34, of which waited for: 18 -> 18; matrix products, arithmetic and copies ran while one was open for 1% -> 2% of each run, Pallas kernels for 0% -> 0%
where the time goes in v1:
time: 512 us; the launch traced here: 508 us
  waiting for transfers between devices  262 us (51%)
  starting transfers between devices  113 us (22%)
  blocking collectives  61.4 us (12%)
  matrix products  39.4 us (8%)
  between operations  15.5 us (3%)
  local copies, waits for them, and re-layouts  10.6 us (2%)
  other arithmetic  6.4 us (1%)
    all_gather x1, waiting for transfers between devices, gather_split(): lax.all_gather(value_rows, ('ctx', 'tile'), axis=0, tiled=True)  163 us
    ppermute x16, starting transfers between devices, extended(): before = lax.ppermute(last, axis, up)  77.3 us
    reduce_scatter x1, waiting for transfers between devices, local(): lax.psum_scatter(partial_value.astype(jnp.bfloat16), 'tile', scatter_dime...  56.8 us
    all_to_all x1, blocking collectives, gather_split(): lax.all_to_all(jnp.stack([key_rows] * lax.axis_size(('ctx', 'tile'))), ('...  41.8 us
    ppermute x16, waiting for transfers between devices, extended(): before = lax.ppermute(last, axis, up)  36.8 us
    ppermute x16, starting transfers between devices, extended(): after = lax.ppermute(first, axis, down)  35.2 us
    all_gather x1, blocking collectives, local(): context_out = lax.all_gather(local_context, 'tile', axis=0, tiled=True)  19.6 us
    dot_general x8, matrix products, advance(): jnp.dot(columns.reshape(patch_rows * patch_cols, 9 * channels), conv_flat...  16.1 us
  transfers between devices with their start and end apart: 34, of which 18 were waited for; matrix products, arithmetic and copies ran while one was open for 2% of the time, Pallas kernels for 0%

profile of v1, /device:TPU:56, one launch (start us, length us, event | category | flops | bytes accessed | tf_op | source)
XLA Modules:
  0.0 507.7 jit_solution(934742488496076673)
XLA Ops:
  8.2 4.6 collective-permute-start
  17.3 4.9 collective-permute-done.1
  24.9 4.5 collective-permute-start.3
  35.8 7.5 %collective-permute-start.4 = (bf16[1,32,512]{2,1,0:T(8,128)(2,1)S(1)}, bf16[1,32,512]{2,1,0:T(8,128)(2,1)S(1)}, u32[]{:S(2)}, u32[]{:S(2)}) collective-permute-start(bf16[1,32,512]{2,1,0:T(8,128)(2,1)S(1)} %get-tuple-element.46), channel_id=1, source_target_pairs={{0,16},{16,32},{32,48},{48,64},{64,80},{80,96},{96,112},{1,17},{17... | collective-permute-start | bytes 98312 | tf_op jit(solution)/shard_map/ppermute | solution.py:19
  44.9 2.9 collective-permute-start.7
  49.8 4.1 collective-permute-done.6
  58.2 8.1 %collective-permute-start.8 = (bf16[1,32,512]{2,1,0:T(8,128)(2,1)S(1)}, bf16[1,32,512]{2,1,0:T(8,128)(2,1)S(1)}, u32[]{:S(2)}, u32[]{:S(2)}) collective-permute-start(bf16[1,32,512]{2,1,0:T(8,128)(2,1)S(1)} %get-tuple-element.44), channel_id=1, source_target_pairs={{0,16},{16,32},{32,48},{48,64},{64,80},{80,96},{96,112},{1,17},{17... | collective-permute-start | bytes 98312 | tf_op jit(solution)/shard_map/ppermute | solution.py:19
  69.9 2.4 collective-permute-start.10
  72.4 3.6 collective-permute-done.10
  81.1 7.8 %collective-permute-start.12 = (bf16[1,32,512]{2,1,0:T(8,128)(2,1)S(1)}, bf16[1,32,512]{2,1,0:T(8,128)(2,1)S(1)}, u32[]{:S(2)}, u32[]{:S(2)}) collective-permute-start(bf16[1,32,512]{2,1,0:T(8,128)(2,1)S(1)} %get-tuple-element.42), channel_id=1, source_target_pairs={{0,16},{16,32},{32,48},{48,64},{64,80},{80,96},{96,112},{1,17},{17... | collective-permute-start | bytes 98312 | tf_op jit(solution)/shard_map/ppermute | solution.py:19
  92.5 2.4 collective-permute-start.14
  95.0 3.5 collective-permute-done.14
  99.7 3.8 fusion.70
  107.3 56.8 %reduce-scatter.2.cloned.1.call-done = bf16[8,1024]{1,0:T(8,128)(2,1)} async-done(((bf16[128,1024]{1,0:T(8,128)(2,1)}), bf16[8,1024]{1,0:T(8,128)(2,1)}) %reduce-scatter.2.cloned.1.call-update) | async-done | bytes 16400 | tf_op jit(solution)/shard_map/reduce_scatter | solution.py:194
  165.8 2.6 convolution_convert_fusion.1
  170.7 41.8 %all_to_all.5 = bf16[128,8,1024]{2,1,0:T(8,128)(2,1)S(1)} all-to-all(bf16[128,8,1024]{2,1,0:T(8,128)(2,1)S(1)} %stack.2), channel_id=1, replica_groups=mesh['ctx'=8,'tile'=16] {'ctx','tile'}, dimensions={0} | all-to-all | bytes 4194304 | tf_op jit(solution)/shard_map/all_to_all | solution.py:207
  214.5 2.6 fusion.178
  217.3 163.0 %all-gather.2.cloned.1.call-done = bf16[1024,1024]{1,0:T(8,128)(2,1)} async-done(((bf16[8,1024]{1,0:T(8,128)(2,1)}), bf16[1024,1024]{1,0:T(8,128)(2,1)}) %all-gather.2.cloned.1.call-update) | async-done | bytes 2097168 | tf_op jit(solution)/shard_map/all_gather | solution.py:215
  380.3 3.2 multiply_reduce_fusion
  383.4 4.8 fusion.87
  388.2 19.6 %all_gather.7 = bf16[128,1024]{1,0:T(8,128)(2,1)S(1)} all-gather(bf16[8,1024]{1,0:T(8,128)(2,1)S(1)} %fusion.87), channel_id=1, replica_groups=mesh['ctx'=8,'tile'=16] {'tile'}, dimensions={0}, use_global_device_ids=true | all-gather | bytes 278528 | tf_op jit(solution)/shard_map/all_gather | solution.py:221
  411.0 7.5 %collective-permute-start.16 = (bf16[1,32,512]{2,1,0:T(8,128)(2,1)S(1)}, bf16[1,32,512]{2,1,0:T(8,128)(2,1)S(1)}, u32[]{:S(2)}, u32[]{:S(2)}) collective-permute-start(bf16[1,32,512]{2,1,0:T(8,128)(2,1)S(1)} %get-tuple-element.40), channel_id=1, source_target_pairs={{0,16},{16,32},{32,48},{48,64},{64,80},{80,96},{96,112},{1,17},{17... | collective-permute-start | bytes 98312 | tf_op jit(solution)/shard_map/ppermute | solution.py:19
  420.2 2.8 collective-permute-start.19
  424.9 4.1 collective-permute-done.18
  429.5 3.9 fusion.68
  435.8 8.1 %collective-permute-start.20 = (bf16[1,32,512]{2,1,0:T(8,128)(2,1)S(1)}, bf16[1,32,512]{2,1,0:T(8,128)(2,1)S(1)}, u32[]{:S(2)}, u32[]{:S(2)}) collective-permute-start(bf16[1,32,512]{2,1,0:T(8,128)(2,1)S(1)} %get-tuple-element.38), channel_id=1, source_target_pairs={{0,16},{16,32},{32,48},{48,64},{64,80},{80,96},{96,112},{1,17},{17... | collective-permute-start | bytes 98312 | tf_op jit(solution)/shard_map/ppermute | solution.py:19
  447.5 2.4 collective-permute-start.22
  450.0 3.6 collective-permute-done.22
  457.9 7.8 %collective-permute-start.24 = (bf16[1,32,512]{2,1,0:T(8,128)(2,1)S(1)}, bf16[1,32,512]{2,1,0:T(8,128)(2,1)S(1)}, u32[]{:S(2)}, u32[]{:S(2)}) collective-permute-start(bf16[1,32,512]{2,1,0:T(8,128)(2,1)S(1)} %get-tuple-element.36), channel_id=1, source_target_pairs={{0,16},{16,32},{32,48},{48,64},{64,80},{80,96},{96,112},{1,17},{17... | collective-permute-start | bytes 98312 | tf_op jit(solution)/shard_map/ppermute | solution.py:19
  471.7 3.6 collective-permute-done.26
  479.6 7.8 %collective-permute-start.28 = (bf16[1,32,512]{2,1,0:T(8,128)(2,1)S(1)}, bf16[1,32,512]{2,1,0:T(8,128)(2,1)S(1)}, u32[]{:S(2)}, u32[]{:S(2)}) collective-permute-start(bf16[1,32,512]{2,1,0:T(8,128)(2,1)S(1)} %get-tuple-element.34), channel_id=1, source_target_pairs={{0,16},{16,32},{32,48},{48,64},{64,80},{80,96},{96,112},{1,17},{17... | collective-permute-start | bytes 98312 | tf_op jit(solution)/shard_map/ppermute | solution.py:19
  493.5 3.6 collective-permute-done.30
  (223 shorter events, 82.5 us)
Async XLA Ops:
  7.2 157.0 %reduce-scatter.2.cloned.1.call-start = ((), (), s32[]{:S(2)}) async-start(), calls=%async_computation.2 | async-start | bytes 278528 | tf_op jit(solution)/shard_map/reduce_scatter | solution.py:194
  8.2 8.1 %collective-permute-start = (bf16[1,32,512]{2,1,0:T(8,128)(2,1)S(1)}, bf16[1,32,512]{2,1,0:T(8,128)(2,1)S(1)}, u32[]{:S(2)}, u32[]{:S(2)}) collective-permute-start(bf16[1,32,512]{2,1,0:T(8,128)(2,1)S(1)} %get-tuple-element.49), channel_id=1, source_target_pairs={{0,16},{16,32},{32,48},{48,64},{64,80},{80,96},{96,112},{1,17},{17... | collective-permute-start | bytes 98312 | tf_op jit(solution)/shard_map/ppermute | solution.py:19
  12.8 9.4 %collective-permute-start.1 = (bf16[1,32,512]{2,1,0:T(8,128)(2,1)S(1)}, bf16[1,32,512]{2,1,0:T(8,128)(2,1)S(1)}, u32[]{:S(2)}, u32[]{:S(2)}) collective-permute-start(bf16[1,32,512]{2,1,0:T(8,128)(2,1)S(1)} %get-tuple-element.48), channel_id=1, source_target_pairs={{16,0},{32,16},{48,32},{64,48},{80,64},{96,80},{112,96},{17,1},{33... | collective-permute-start | bytes 98312 | tf_op jit(solution)/shard_map/ppermute | solution.py:20
  22.2 7.2 %collective-permute-start.2 = (bf16[10,1,512]{2,1,0:T(2,128)(2,1)S(1)}, bf16[10,1,512]{2,1,0:T(2,128)(2,1)S(1)}, u32[]{:S(2)}, u32[]{:S(2)}) collective-permute-start(bf16[10,1,512]{2,1,0:T(2,128)(2,1)S(1)} %get-tuple-element.33), channel_id=1, source_target_pairs={{0,1},{1,2},{2,3},{3,4},{4,5},{5,6},{6,7},{7,8},{8,9},{9,10},{10,1... | collective-permute-start | bytes 30728 | tf_op jit(solution)/shard_map/ppermute | solution.py:19
  24.9 6.0 %collective-permute-start.3 = (bf16[10,1,512]{2,1,0:T(2,128)(2,1)S(1)}, bf16[10,1,512]{2,1,0:T(2,128)(2,1)S(1)}, u32[]{:S(2)}, u32[]{:S(2)}) collective-permute-start(bf16[10,1,512]{2,1,0:T(2,128)(2,1)S(1)} %get-tuple-element.32), channel_id=1, source_target_pairs={{1,0},{2,1},{3,2},{4,3},{5,4},{6,5},{7,6},{8,7},{9,8},{10,9},{11,1... | collective-permute-start | bytes 30728 | tf_op jit(solution)/shard_map/ppermute | solution.py:20
  33.8 9.5 %collective-permute-start.5 = (bf16[1,32,512]{2,1,0:T(8,128)(2,1)S(1)}, bf16[1,32,512]{2,1,0:T(8,128)(2,1)S(1)}, u32[]{:S(2)}, u32[]{:S(2)}) collective-permute-start(bf16[1,32,512]{2,1,0:T(8,128)(2,1)S(1)} %get-tuple-element.47), channel_id=1, source_target_pairs={{16,0},{32,16},{48,32},{64,48},{80,64},{96,80},{112,96},{17,1},{33... | collective-permute-start | bytes 98312 | tf_op jit(solution)/shard_map/ppermute | solution.py:20
  35.8 9.1 %collective-permute-start.4 = (bf16[1,32,512]{2,1,0:T(8,128)(2,1)S(1)}, bf16[1,32,512]{2,1,0:T(8,128)(2,1)S(1)}, u32[]{:S(2)}, u32[]{:S(2)}) collective-permute-start(bf16[1,32,512]{2,1,0:T(8,128)(2,1)S(1)} %get-tuple-element.46), channel_id=1, source_target_pairs={{0,16},{16,32},{32,48},{48,64},{64,80},{80,96},{96,112},{1,17},{17... | collective-permute-start | bytes 98312 | tf_op jit(solution)/shard_map/ppermute | solution.py:19
  44.9 4.9 collective-permute-start.7
  47.9 6.0 %collective-permute-start.6 = (bf16[10,1,512]{2,1,0:T(2,128)(2,1)S(1)}, bf16[10,1,512]{2,1,0:T(2,128)(2,1)S(1)}, u32[]{:S(2)}, u32[]{:S(2)}) collective-permute-start(bf16[10,1,512]{2,1,0:T(2,128)(2,1)S(1)} %get-tuple-element.31), channel_id=1, source_target_pairs={{0,1},{1,2},{2,3},{3,4},{4,5},{5,6},{6,7},{7,8},{8,9},{9,10},{10,1... | collective-permute-start | bytes 30728 | tf_op jit(solution)/shard_map/ppermute | solution.py:19
  56.3 10.1 %collective-permute-start.9 = (bf16[1,32,512]{2,1,0:T(8,128)(2,1)S(1)}, bf16[1,32,512]{2,1,0:T(8,128)(2,1)S(1)}, u32[]{:S(2)}, u32[]{:S(2)}) collective-permute-start(bf16[1,32,512]{2,1,0:T(8,128)(2,1)S(1)} %get-tuple-element.45), channel_id=1, source_target_pairs={{16,0},{32,16},{48,32},{64,48},{80,64},{96,80},{112,96},{17,1},{33... | collective-permute-start | bytes 98312 | tf_op jit(solution)/shard_map/ppermute | solution.py:20
  58.2 9.7 %collective-permute-start.8 = (bf16[1,32,512]{2,1,0:T(8,128)(2,1)S(1)}, bf16[1,32,512]{2,1,0:T(8,128)(2,1)S(1)}, u32[]{:S(2)}, u32[]{:S(2)}) collective-permute-start(bf16[1,32,512]{2,1,0:T(8,128)(2,1)S(1)} %get-tuple-element.44), channel_id=1, source_target_pairs={{0,16},{16,32},{32,48},{48,64},{64,80},{80,96},{96,112},{1,17},{17... | collective-permute-start | bytes 98312 | tf_op jit(solution)/shard_map/ppermute | solution.py:19
  68.0 4.4 collective-permute-start.11
  69.9 6.0 %collective-permute-start.10 = (bf16[10,1,512]{2,1,0:T(2,128)(2,1)S(1)}, bf16[10,1,512]{2,1,0:T(2,128)(2,1)S(1)}, u32[]{:S(2)}, u32[]{:S(2)}) collective-permute-start(bf16[10,1,512]{2,1,0:T(2,128)(2,1)S(1)} %get-tuple-element.27), channel_id=1, source_target_pairs={{0,1},{1,2},{2,3},{3,4},{4,5},{5,6},{6,7},{7,8},{8,9},{9,10},{10,1... | collective-permute-start | bytes 30728 | tf_op jit(solution)/shard_map/ppermute | solution.py:19
  79.2 9.8 %collective-permute-start.13 = (bf16[1,32,512]{2,1,0:T(8,128)(2,1)S(1)}, bf16[1,32,512]{2,1,0:T(8,128)(2,1)S(1)}, u32[]{:S(2)}, u32[]{:S(2)}) collective-permute-start(bf16[1,32,512]{2,1,0:T(8,128)(2,1)S(1)} %get-tuple-element.43), channel_id=1, source_target_pairs={{16,0},{32,16},{48,32},{64,48},{80,64},{96,80},{112,96},{17,1},{33... | collective-permute-start | bytes 98312 | tf_op jit(solution)/shard_map/ppermute | solution.py:20
  81.1 9.4 %collective-permute-start.12 = (bf16[1,32,512]{2,1,0:T(8,128)(2,1)S(1)}, bf16[1,32,512]{2,1,0:T(8,128)(2,1)S(1)}, u32[]{:S(2)}, u32[]{:S(2)}) collective-permute-start(bf16[1,32,512]{2,1,0:T(8,128)(2,1)S(1)} %get-tuple-element.42), channel_id=1, source_target_pairs={{0,16},{16,32},{32,48},{48,64},{64,80},{80,96},{96,112},{1,17},{17... | collective-permute-start | bytes 98312 | tf_op jit(solution)/shard_map/ppermute | solution.py:19
  90.5 4.4 collective-permute-start.15
  92.5 6.0 %collective-permute-start.14 = (bf16[10,1,512]{2,1,0:T(2,128)(2,1)S(1)}, bf16[10,1,512]{2,1,0:T(2,128)(2,1)S(1)}, u32[]{:S(2)}, u32[]{:S(2)}) collective-permute-start(bf16[10,1,512]{2,1,0:T(2,128)(2,1)S(1)} %get-tuple-element.23), channel_id=1, source_target_pairs={{0,1},{1,2},{2,3},{3,4},{4,5},{5,6},{6,7},{7,8},{8,9},{9,10},{10,1... | collective-permute-start | bytes 30728 | tf_op jit(solution)/shard_map/ppermute | solution.py:19
  107.3 273.0 %all-gather.2.cloned.1.call-start = ((), (), s32[]{:S(2)}) async-start(), calls=%async_computation.3 | async-start | bytes 2113536 | tf_op jit(solution)/shard_map/all_gather | solution.py:215
  409.1 9.5 %collective-permute-start.17 = (bf16[1,32,512]{2,1,0:T(8,128)(2,1)S(1)}, bf16[1,32,512]{2,1,0:T(8,128)(2,1)S(1)}, u32[]{:S(2)}, u32[]{:S(2)}) collective-permute-start(bf16[1,32,512]{2,1,0:T(8,128)(2,1)S(1)} %get-tuple-element.41), channel_id=1, source_target_pairs={{16,0},{32,16},{48,32},{64,48},{80,64},{96,80},{112,96},{17,1},{33... | collective-permute-start | bytes 98312 | tf_op jit(solution)/shard_map/ppermute | solution.py:20
  411.0 9.1 %collective-permute-start.16 = (bf16[1,32,512]{2,1,0:T(8,128)(2,1)S(1)}, bf16[1,32,512]{2,1,0:T(8,128)(2,1)S(1)}, u32[]{:S(2)}, u32[]{:S(2)}) collective-permute-start(bf16[1,32,512]{2,1,0:T(8,128)(2,1)S(1)} %get-tuple-element.40), channel_id=1, source_target_pairs={{0,16},{16,32},{32,48},{48,64},{64,80},{80,96},{96,112},{1,17},{17... | collective-permute-start | bytes 98312 | tf_op jit(solution)/shard_map/ppermute | solution.py:19
  420.2 4.8 collective-permute-start.19
  423.0 6.0 %collective-permute-start.18 = (bf16[10,1,512]{2,1,0:T(2,128)(2,1)S(1)}, bf16[10,1,512]{2,1,0:T(2,128)(2,1)S(1)}, u32[]{:S(2)}, u32[]{:S(2)}) collective-permute-start(bf16[10,1,512]{2,1,0:T(2,128)(2,1)S(1)} %get-tuple-element.19), channel_id=1, source_target_pairs={{0,1},{1,2},{2,3},{3,4},{4,5},{5,6},{6,7},{7,8},{8,9},{9,10},{10,1... | collective-permute-start | bytes 30728 | tf_op jit(solution)/shard_map/ppermute | solution.py:19
  433.9 10.1 %collective-permute-start.21 = (bf16[1,32,512]{2,1,0:T(8,128)(2,1)S(1)}, bf16[1,32,512]{2,1,0:T(8,128)(2,1)S(1)}, u32[]{:S(2)}, u32[]{:S(2)}) collective-permute-start(bf16[1,32,512]{2,1,0:T(8,128)(2,1)S(1)} %get-tuple-element.39), channel_id=1, source_target_pairs={{16,0},{32,16},{48,32},{64,48},{80,64},{96,80},{112,96},{17,1},{33... | collective-permute-start | bytes 98312 | tf_op jit(solution)/shard_map/ppermute | solution.py:20
  435.8 9.7 %collective-permute-start.20 = (bf16[1,32,512]{2,1,0:T(8,128)(2,1)S(1)}, bf16[1,32,512]{2,1,0:T(8,128)(2,1)S(1)}, u32[]{:S(2)}, u32[]{:S(2)}) collective-permute-start(bf16[1,32,512]{2,1,0:T(8,128)(2,1)S(1)} %get-tuple-element.38), channel_id=1, source_target_pairs={{0,16},{16,32},{32,48},{48,64},{64,80},{80,96},{96,112},{1,17},{17... | collective-permute-start | bytes 98312 | tf_op jit(solution)/shard_map/ppermute | solution.py:19
  445.6 4.4 collective-permute-start.23
  447.5 6.0 %collective-permute-start.22 = (bf16[10,1,512]{2,1,0:T(2,128)(2,1)S(1)}, bf16[10,1,512]{2,1,0:T(2,128)(2,1)S(1)}, u32[]{:S(2)}, u32[]{:S(2)}) collective-permute-start(bf16[10,1,512]{2,1,0:T(2,128)(2,1)S(1)} %get-tuple-element.15), channel_id=1, source_target_pairs={{0,1},{1,2},{2,3},{3,4},{4,5},{5,6},{6,7},{7,8},{8,9},{9,10},{10,1... | collective-permute-start | bytes 30728 | tf_op jit(solution)/shard_map/ppermute | solution.py:19
  456.0 9.8 %collective-permute-start.25 = (bf16[1,32,512]{2,1,0:T(8,128)(2,1)S(1)}, bf16[1,32,512]{2,1,0:T(8,128)(2,1)S(1)}, u32[]{:S(2)}, u32[]{:S(2)}) collective-permute-start(bf16[1,32,512]{2,1,0:T(8,128)(2,1)S(1)} %get-tuple-element.37), channel_id=1, source_target_pairs={{16,0},{32,16},{48,32},{64,48},{80,64},{96,80},{112,96},{17,1},{33... | collective-permute-start | bytes 98312 | tf_op jit(solution)/shard_map/ppermute | solution.py:20
  457.9 9.4 %collective-permute-start.24 = (bf16[1,32,512]{2,1,0:T(8,128)(2,1)S(1)}, bf16[1,32,512]{2,1,0:T(8,128)(2,1)S(1)}, u32[]{:S(2)}, u32[]{:S(2)}) collective-permute-start(bf16[1,32,512]{2,1,0:T(8,128)(2,1)S(1)} %get-tuple-element.36), channel_id=1, source_target_pairs={{0,16},{16,32},{32,48},{48,64},{64,80},{80,96},{96,112},{1,17},{17... | collective-permute-start | bytes 98312 | tf_op jit(solution)/shard_map/ppermute | solution.py:19
  469.3 6.0 %collective-permute-start.26 = (bf16[10,1,512]{2,1,0:T(2,128)(2,1)S(1)}, bf16[10,1,512]{2,1,0:T(2,128)(2,1)S(1)}, u32[]{:S(2)}, u32[]{:S(2)}) collective-permute-start(bf16[10,1,512]{2,1,0:T(2,128)(2,1)S(1)} %get-tuple-element.11), channel_id=1, source_target_pairs={{0,1},{1,2},{2,3},{3,4},{4,5},{5,6},{6,7},{7,8},{8,9},{9,10},{10,1... | collective-permute-start | bytes 30728 | tf_op jit(solution)/shard_map/ppermute | solution.py:19
  477.7 9.8 %collective-permute-start.29 = (bf16[1,32,512]{2,1,0:T(8,128)(2,1)S(1)}, bf16[1,32,512]{2,1,0:T(8,128)(2,1)S(1)}, u32[]{:S(2)}, u32[]{:S(2)}) collective-permute-start(bf16[1,32,512]{2,1,0:T(8,128)(2,1)S(1)} %get-tuple-element.35), channel_id=1, source_target_pairs={{16,0},{32,16},{48,32},{64,48},{80,64},{96,80},{112,96},{17,1},{33... | collective-permute-start | bytes 98312 | tf_op jit(solution)/shard_map/ppermute | solution.py:20
  479.6 9.4 %collective-permute-start.28 = (bf16[1,32,512]{2,1,0:T(8,128)(2,1)S(1)}, bf16[1,32,512]{2,1,0:T(8,128)(2,1)S(1)}, u32[]{:S(2)}, u32[]{:S(2)}) collective-permute-start(bf16[1,32,512]{2,1,0:T(8,128)(2,1)S(1)} %get-tuple-element.34), channel_id=1, source_target_pairs={{0,16},{16,32},{32,48},{48,64},{64,80},{80,96},{96,112},{1,17},{17... | collective-permute-start | bytes 98312 | tf_op jit(solution)/shard_map/ppermute | solution.py:19
  491.0 6.0 %collective-permute-start.30 = (bf16[10,1,512]{2,1,0:T(2,128)(2,1)S(1)}, bf16[10,1,512]{2,1,0:T(2,128)(2,1)S(1)}, u32[]{:S(2)}, u32[]{:S(2)}) collective-permute-start(bf16[10,1,512]{2,1,0:T(2,128)(2,1)S(1)} %get-tuple-element.7), channel_id=1, source_target_pairs={{0,1},{1,2},{2,3},{3,4},{4,5},{5,6},{6,7},{7,8},{8,9},{9,10},{10,1... | collective-permute-start | bytes 30728 | tf_op jit(solution)/shard_map/ppermute | solution.py:19
  (18 other events, 737.1 us)
Sparse Core Ops, SparseCore 0:
  107.4 56.7 reduce-scatter.1
  168.6 211.6 all-gather.1
